TPU v7x, 256 devices: a whole 4x4x8 slice. The times are simulated.
256 devices in a mesh: dp: 8 (over x, core), ctx: 32 (over z, y).
Axes of the slice: x: 4, y: 4, z: 8, core: 2. Of those that a mesh axis runs over, the one named last changes fastest.
Arguments:
- tokens: bfloat16 [8, 4096, 4096], P('dp', 'ctx'), may hold values from -6 to 6
- qk_weight: bfloat16 [4096, 512], replicated, may hold values from -0.09375 to 0.09375
- conv_weight: float32 [3, 512], replicated, may hold values from -3 to 3
- values: bfloat16 [8, 4096, 2048], P('dp', 'ctx'), may hold values from -6 to 6
- cotangent: bfloat16 [8, 4096, 2048], P('dp', 'ctx'), may hold values from -6 to 6
Outputs:
- mixed_out: bfloat16 [8, 4096, 2048], P('dp', 'ctx')
- grad_tokens: bfloat16 [8, 4096, 4096], P('dp', 'ctx')
- grad_values: bfloat16 [8, 4096, 2048], P('dp', 'ctx')
- grad_qk_weight: float32 [4096, 512], P('ctx')
All inputs are finite; a program needn't handle non-finite values.
Results may differ from a plain program's by a relative error of at most 0.04.
Values sent between devices are 32-bit elements; how exact they have to be, the bound alone decides.
No kernel may reach another device: no remote copies, remote signals or barrier semaphores. Data moves between devices by JAX's collectives and lax.ppermute only.
A program may use at most 128 MiB of HBM per device.

v0:
```python
import jax
import jax.numpy as jnp
import numpy as np
from jax import lax
from jax.sharding import PartitionSpec as P

H = 16
F = 16
V = 128


def passed_along(value, axis, steps):
    count = lax.axis_size(axis)
    first, last = (max(0, -steps), min(count, count - steps))
    return lax.ppermute(value, axis, [(source, source + steps) for source in range(first, last)])


def entering(part, axis, combine, identity, reverse):
    count = lax.axis_size(axis)
    place = lax.axis_index(axis)
    ahead = count - 1 - place if reverse else place
    gathered = jax.tree.map(lambda a: lax.all_gather(a, axis), part)
    state = jax.tree.map(lambda a, e: jnp.zeros_like(a) + jnp.asarray(e, a.dtype), part, identity)

    def one(lap, state):
        source = count - 1 - lap if reverse else lap
        return combine(
            state, jax.tree.map(lambda a: lax.dynamic_index_in_dim(a, source, 0, False), gathered)
        )

    return lax.fori_loop(0, ahead, one, state)


def product(form, left, right):
    return jnp.einsum(form, left, right, preferred_element_type=jnp.float32)


def taylor_map(inputs):
    size = inputs.shape[1]
    pieces = [jnp.ones_like(inputs[:, :1]), inputs * size ** (-0.25)]
    for first in range(size):
        scale = np.full((size - first, 1), 1.0 / np.sqrt(size), np.float32)
        scale[0, 0] = 1.0 / np.sqrt(2.0 * size)
        pieces.append(inputs[:, first : first + 1] * inputs[:, first:] * scale)
    return jnp.concatenate(pieces, 1).astype(jnp.bfloat16)


def features_of(extended, conv_weight):
    taps = conv_weight.shape[0]
    length = extended.shape[0] - taps + 1
    mixed = conv_weight[0] * extended[taps - 1 :]
    for offset in range(1, taps):
        mixed = (
            mixed + conv_weight[offset] * extended[taps - 1 - offset : taps - 1 - offset + length]
        )
    half = mixed.shape[1] // 2
    query = jnp.transpose(mixed[:, :half].reshape(length, H, F), (1, 2, 0))
    key_part = jnp.transpose(mixed[:, half:].reshape(length, H, F), (1, 2, 0))
    return (taylor_map(query), taylor_map(key_part))


def block_state(key_feat, values32):
    values_bf = values32.astype(jnp.bfloat16)
    state = product("het,thv->hev", key_feat, values_bf)
    return (state, jnp.sum(key_feat.astype(jnp.float32), -1))


def block_output(query_feat, key_feat, values32, carried, carried_total):
    length = query_feat.shape[-1]
    values_bf = values32.astype(jnp.bfloat16)
    causal = jnp.tril(jnp.ones((length, length), jnp.float32))
    scores = product("het,hes->hts", query_feat, key_feat) * causal
    local_sum = jnp.sum(scores, -1)
    numer = product("hts,shv->thv", scores.astype(jnp.bfloat16), values_bf)
    numer = numer + product("het,hev->thv", query_feat, carried.astype(jnp.bfloat16))
    denom = jnp.transpose(local_sum) + jnp.einsum(
        "het,he->th", query_feat.astype(jnp.float32), carried_total, precision=lax.Precision.HIGHEST
    )
    return (numer / denom[..., None]).reshape(length, -1)


def add_pair(earlier, later):
    return (earlier[0] + later[0], earlier[1] + later[1])


def on_device(tokens, qk_weight, conv_weight, values, cotangent):
    local_x = tokens[0]
    row_count = local_x.shape[0]
    taps = conv_weight.shape[0]
    projected = jnp.dot(local_x, qk_weight, preferred_element_type=jnp.float32)
    borrowed = passed_along(projected[row_count - taps + 1 :], "ctx", 1)
    extended = jnp.concatenate([borrowed, projected], 0)
    values32 = values[0].reshape(row_count, H, V).astype(jnp.float32)
    (query_feat, key_feat), back_features = jax.vjp(
        lambda ext_in: features_of(ext_in, conv_weight), extended
    )
    (states, totals), back_state = jax.vjp(block_state, key_feat, values32)
    identity = (jnp.zeros_like(states), jnp.zeros_like(totals))
    carried, carried_total = entering((states, totals), "ctx", add_pair, identity, False)
    result, back_output = jax.vjp(
        block_output, query_feat, key_feat, values32, carried, carried_total
    )
    grad_query, grad_key_out, grad_vals_out, grad_carried, grad_total = back_output(
        cotangent[0].astype(jnp.float32)
    )
    grad_states, grad_totals = entering((grad_carried, grad_total), "ctx", add_pair, identity, True)
    grad_key_state, grad_vals_state = back_state((grad_states, grad_totals))
    (grad_extended,) = back_features((grad_query, grad_key_out + grad_key_state))
    returned = passed_along(grad_extended[: taps - 1], "ctx", -1)
    grad_proj = grad_extended[taps - 1 :]
    grad_proj = grad_proj.at[row_count - taps + 1 :].add(returned)
    grad_bf = grad_proj.astype(jnp.bfloat16)
    grad_x = lax.dot_general(
        grad_bf, qk_weight, (((1,), (1,)), ((), ())), preferred_element_type=jnp.float32
    ).astype(jnp.bfloat16)
    grad_vals = (grad_vals_out + grad_vals_state).reshape(row_count, H * V).astype(jnp.bfloat16)
    partial_rows = lax.psum_scatter(
        lax.dot_general(
            local_x, grad_bf, (((0,), (0,)), ((), ())), preferred_element_type=jnp.float32
        ),
        "ctx",
        scatter_dimension=0,
        tiled=True,
    )
    weight_grad = lax.psum(partial_rows, "dp")
    return (result.astype(jnp.bfloat16)[None], grad_x[None], grad_vals[None], weight_grad)


def solution(mesh):
    return jax.shard_map(
        on_device,
        mesh=mesh,
        in_specs=(P("dp", "ctx", None), P(), P(), P("dp", "ctx", None), P("dp", "ctx", None)),
        out_specs=(
            P("dp", "ctx", None),
            P("dp", "ctx", None),
            P("dp", "ctx", None),
            P("ctx", None),
        ),
        check_vma=False,
    )
```

profile of v0, /device:TPU:8, one launch (start us, length us, event | category | flops | bytes accessed | tf_op | source)
XLA Modules:
  0.0 1105.6 jit_solution(4012632791400076872)
XLA Ops:
  8.4 3.0 fusion.18
  11.4 3.5 collective-permute-start
  15.1 1.8 collective-permute-done
  20.2 1.9 copy.231
  24.8 57.4 %all-gather.1 = f32[512,153]{1,0:T(8,128)} all-gather(f32[16,153]{1,0:T(8,128)S(1)} %copy.232), channel_id=3, replica_groups=mesh['dp'=8,'ctx'=32] {'ctx'}, dimensions={0}, use_global_device_ids=true | all-gather | bytes 323136 | tf_op jit(solution)/shard_map/all_gather | solution.py:22
  83.5 225.5 %all-gather.7.cloned.1.call-done = f32[512,153,128]{2,0,1:T(8,128)} async-done(((f32[16,153,128]{2,0,1:T(8,128)}), f32[512,153,128]{2,0,1:T(8,128)}) %all-gather.7.cloned.1.call-update) | async-done | bytes 40108048 | tf_op jit(solution)/shard_map/all_gather | solution.py:22
  309.2 2.8 while.27
  309.2 1.4 constant_dynamic-slice_fusion.4
  312.0 1.7 fusion.38
  313.7 1.9 fusion.4
  315.6 1.8 copy.243
  318.2 1.7 convolution_bitcast_fusion.2
  322.3 136.5 %all-gather.3 = f32[512,153]{1,0:T(8,128)} all-gather(f32[16,153]{1,0:T(8,128)S(1)} %bitcast.226), channel_id=5, replica_groups=mesh['dp'=8,'ctx'=32] {'ctx'}, dimensions={0}, use_global_device_ids=true | all-gather | bytes 323136 | tf_op jit(solution)/shard_map/all_gather | solution.py:22
  463.9 219.0 %all-gather.9.cloned.1.call-done = f32[512,153,128]{2,0,1:T(8,128)} async-done(((f32[16,153,128]{2,0,1:T(8,128)}), f32[512,153,128]{2,0,1:T(8,128)}) %all-gather.9.cloned.1.call-update) | async-done | bytes 40108048 | tf_op jit(solution)/shard_map/all_gather | solution.py:22
  683.1 83.5 %while.28 = (s32[]{:T(128)}, f32[16,153,128]{2,1,0:T(8,128)S(1)}, f32[16,153]{1,0:T(8,128)S(1)}, s32[]{:T(128)}, f32[32,16,153,128]{3,1,0,2:T(8,128)}, /*index=5...) while((s32[]{:T(128)}, f32[16,153,128]{2,1,0:T(8,128)S(1)}, f32[16,153]{1,0:T(8,128)S(1)}, ...), condition=%wide.region_6.7_spmd, body=%wide.region_5.6_spmd.sunk | while | flops 315798 | bytes 6296419 | solution.py:31
  683.3 1.4 constant_dynamic-slice_fusion.5
  686.1 1.4 constant_dynamic-slice_fusion.5
  688.9 1.4 constant_dynamic-slice_fusion.5
  691.7 1.4 constant_dynamic-slice_fusion.5
  694.4 1.4 constant_dynamic-slice_fusion.5
  697.2 1.4 constant_dynamic-slice_fusion.5
  700.0 1.4 constant_dynamic-slice_fusion.5
  702.8 1.4 constant_dynamic-slice_fusion.5
  705.5 1.4 constant_dynamic-slice_fusion.5
  708.3 1.4 constant_dynamic-slice_fusion.5
  711.1 1.4 constant_dynamic-slice_fusion.5
  713.9 1.4 constant_dynamic-slice_fusion.5
  716.6 1.4 constant_dynamic-slice_fusion.5
  719.4 1.4 constant_dynamic-slice_fusion.5
  722.2 1.4 constant_dynamic-slice_fusion.5
  725.0 1.4 constant_dynamic-slice_fusion.5
  727.8 1.4 constant_dynamic-slice_fusion.5
  730.5 1.4 constant_dynamic-slice_fusion.5
  733.3 1.4 constant_dynamic-slice_fusion.5
  736.1 1.4 constant_dynamic-slice_fusion.5
  738.9 1.4 constant_dynamic-slice_fusion.5
  741.6 1.4 constant_dynamic-slice_fusion.5
  744.4 1.4 constant_dynamic-slice_fusion.5
  766.6 2.4 fusion.42
  770.5 1.9 fusion.24
  790.9 1.4 fusion.61
  793.3 6.8 collective-permute-start.1
  801.4 4.6 convolution_bitcast_fusion
  806.1 2.0 copy.259
  811.0 219.9 %reduce-scatter.2.cloned.1.call-done = f32[128,512]{0,1:T(8,128)} async-done(((f32[4096,512]{0,1:T(8,128)}), f32[128,512]{0,1:T(8,128)}) %reduce-scatter.2.cloned.1.call-update) | async-done | bytes 262160 | tf_op jit(solution)/shard_map/reduce_scatter | solution.py:117
  1030.9 4.6 fusion.2
  1035.5 61.8 %all-reduce.67.cloned.1.call-done = f32[128,512]{0,1:T(8,128)} async-done(((f32[128,512]{0,1:T(8,128)}), f32[128,512]{0,1:T(8,128)}) %all-reduce.67.cloned.1.call-update) | async-done | bytes 262160 | tf_op jit(solution)/shard_map/psum | solution.py:125
  1097.3 1.8 copy.261
  (385 shorter events, 93.5 us)
Async XLA Ops:
  7.2 7.7 copy-start.81
  7.2 301.8 %all-gather.7.cloned.1.call-start = ((), (), s32[]{:S(2)}) async-start(), calls=%async_computation.3 | async-start | bytes 41361408 | tf_op jit(solution)/shard_map/all_gather | solution.py:22
  8.4 6.5 copy-start.11
  11.4 5.5 collective-permute-start
  15.1 4.8 copy-start.6
  22.1 660.9 %all-gather.9.cloned.1.call-start = ((), (), s32[]{:S(2)}) async-start(), calls=%async_computation.4 | async-start | bytes 41361408 | tf_op jit(solution)/shard_map/all_gather | solution.py:22
  24.3 59.2 %copy-start.72 = (f32[128,128]{0,1:T(8,128)}, f32[128,128]{0,1:T(8,128)S(1)}, u32[]{:S(2)}) copy-start(f32[128,128]{0,1:T(8,128)S(1)} %fusion.76) | copy-start | bytes 196612
  82.1 226.9 %copy-start.1 = (bf16[16,153,128]{2,0,1:T(8,128)(2,1)}, bf16[16,153,128]{2,0,1:T(8,128)(2,1)S(1)}, u32[]{:S(2)}) copy-start(bf16[16,153,128]{2,0,1:T(8,128)(2,1)S(1)} %constant_dynamic-update-slice_fusion) | copy-start | bytes 1880068
  313.7 145.8 %copy-start.79 = (f32[128,16]{0,1:T(8,128)}, f32[128,16]{0,1:T(8,128)S(1)}, u32[]{:S(2)}) copy-start(f32[128,16]{0,1:T(8,128)S(1)} %get-tuple-element.278) | copy-start | bytes 24580
  317.4 713.5 %reduce-scatter.2.cloned.1.call-start = ((), (), s32[]{:S(2)}) async-start(), calls=%async_computation.1 | async-start | bytes 8650752 | tf_op jit(solution)/shard_map/reduce_scatter | solution.py:117
  321.2 137.6 %copy-start.73 = (f32[128,128]{0,1:T(8,128)S(1)}, f32[128,128]{0,1:T(8,128)}, u32[]{:S(2)}) copy-start(f32[128,128]{0,1:T(8,128)} %copy-done.72) | copy-start | bytes 196612
  772.4 17.7 %copy-start.5 = (f32[16,153,128]{2,0,1:T(8,128)}, f32[16,153,128]{2,0,1:T(8,128)S(1)}, u32[]{:S(2)}) copy-start(f32[16,153,128]{2,0,1:T(8,128)S(1)} %fusion.24) | copy-start | bytes 3760132
  772.4 3.6 copy-start.19
  772.4 3.6 copy-start.25
  773.2 4.2 copy-start.65
  773.2 4.2 copy-start.67
  773.2 4.2 copy-start.105
  773.9 4.9 copy-start.17
  773.9 4.9 copy-start.21
  773.9 4.9 copy-start.99
  774.7 5.6 copy-start.47
  774.7 5.6 copy-start.51
  774.7 5.5 copy-start.97
  776.0 5.6 copy-start.69
  776.0 5.6 copy-start.71
  776.1 5.6 copy-start.95
  776.1 6.2 copy-start.41
  776.1 6.2 copy-start.49
  776.1 6.2 copy-start.93
  777.4 6.2 copy-start.39
  777.4 6.2 copy-start.45
  777.5 6.2 copy-start.91
  777.5 7.4 copy-start.37
  777.5 7.4 copy-start.43
  777.5 7.4 copy-start.89
  778.8 7.4 copy-start.33
  778.8 7.4 copy-start.35
  778.8 7.3 copy-start.87
  778.9 8.6 copy-start.59
  778.9 8.6 copy-start.63
  778.9 8.6 copy-start.85
  780.2 8.5 copy-start.57
  780.2 8.5 copy-start.61
  780.2 8.5 copy-start.83
  780.3 10.4 copy-start.15
  780.3 10.4 copy-start.74
  793.3 8.1 collective-permute-start.1
  806.0 291.2 %all-reduce.67.cloned.1.call-start = ((), (), s32[]{:S(2)}) async-start(), calls=%async_computation.2 | async-start | bytes 524288 | tf_op jit(solution)/shard_map/psum | solution.py:125
  (70 other events, 108.2 us)
Sparse Core Ops, SparseCore 0:
  22.2 286.7 all-gather.6
  317.5 365.3 all-gather.8
  806.2 224.6 reduce-scatter.1
  1033.1 64.1 all-reduce.66
where the time goes:
time: 1110 us
  waiting for transfers between devices  729 us (66%)
  blocking collectives  194 us (17%)
  other arithmetic  68.4 us (6%)
  local copies, waits for them, and re-layouts  60.7 us (5%)
  matrix products  27.2 us (2%)
  between operations  15.3 us (1%)
    all_gather x2, waiting for transfers between devices, entering(): gathered = jax.tree.map(lambda a: lax.all_gather(a, axis), part)  445 us
    reduce_scatter x1, waiting for transfers between devices, on_device(): lax.psum_scatter(lax.dot_general(local_x, grad_bf, (((0,), (0,)), ((), ()...  220 us
    all_gather x2, blocking collectives, entering(): gathered = jax.tree.map(lambda a: lax.all_gather(a, axis), part)  194 us
    psum x1, waiting for transfers between devices, on_device(): weight_grad = lax.psum(partial_rows, 'dp')  61.8 us
    dynamic_slice x31, local copies, waits for them, and re-layouts, one(): lax.dynamic_index_in_dim(a, source, 0, False)  43.3 us
    add x62, other arithmetic, add_pair(): return (earlier[0] + later[0], earlier[1] + later[1])  42.6 us
  transfers between devices with their start and end apart: 6, of which 6 were waited for; matrix products, arithmetic and copies ran while one was open for 2% of the time, Pallas kernels for 0%

commit v1 on v0

--- a/solution.py
+++ b/solution.py
@@ -122,7 +122,11 @@
         scatter_dimension=0,
         tiled=True,
     )
-    weight_grad = lax.psum(partial_rows, "dp")
+    weight_grad = partial_rows
+    for hop in (1, 2, 4):
+        weight_grad = weight_grad + lax.ppermute(
+            weight_grad, "dp", [(dev, dev ^ hop) for dev in range(8)]
+        )
     return (result.astype(jnp.bfloat16)[None], grad_x[None], grad_vals[None], weight_grad)
 
 

time: 1110 us -> 1060 us (0.955)
  waiting for transfers between devices: 729 us -> 679 us
    psum x1 -> x0, waiting for transfers between devices: 61.8 us -> none  [on_device(): weight_grad = lax.psum(partial_rows, 'dp')]
  transfers between devices with their start and end apart: 6 -> 8, of which waited for: 6 -> 8; matrix products, arithmetic and copies ran while one was open for 2% -> 2% of each run, Pallas kernels for 0% -> 0%
where the time goes in v1:
time: 1060 us
  waiting for transfers between devices  679 us (64%)
  blocking collectives  194 us (18%)
  other arithmetic  69.1 us (7%)
  local copies, waits for them, and re-layouts  58.9 us (6%)
  matrix products  27.2 us (3%)
  between operations  15.3 us (1%)
  starting transfers between devices  15 us (1%)
    all_gather x2, waiting for transfers between devices, entering(): gathered = jax.tree.map(lambda a: lax.all_gather(a, axis), part)  446 us
    reduce_scatter x1, waiting for transfers between devices, on_device(): lax.psum_scatter(lax.dot_general(local_x, grad_bf, (((0,), (0,)), ((), ()...  223 us
    all_gather x2, blocking collectives, entering(): gathered = jax.tree.map(lambda a: lax.all_gather(a, axis), part)  194 us
    dynamic_slice x31, local copies, waits for them, and re-layouts, one(): lax.dynamic_index_in_dim(a, source, 0, False)  43.3 us
    add x62, other arithmetic, add_pair(): return (earlier[0] + later[0], earlier[1] + later[1])  42.6 us
  transfers between devices with their start and end apart: 8, of which 8 were waited for; matrix products, arithmetic and copies ran while one was open for 2% of the time, Pallas kernels for 0%

profile of v1, /device:TPU:8, one launch (start us, length us, event | category | flops | bytes accessed | tf_op | source)
XLA Modules:
  0.0 1058.8 jit_solution(17442905040304585244)
XLA Ops:
  8.4 3.0 fusion.18
  11.4 3.5 collective-permute-start
  15.1 1.8 collective-permute-done
  20.2 1.8 copy.231
  24.7 57.3 %all-gather.1 = f32[512,153]{1,0:T(8,128)} all-gather(f32[16,153]{1,0:T(8,128)S(1)} %copy.232), channel_id=3, replica_groups=mesh['dp'=8,'ctx'=32] {'ctx'}, dimensions={0}, use_global_device_ids=true | all-gather | bytes 323136 | tf_op jit(solution)/shard_map/all_gather | solution.py:22
  83.4 226.1 %all-gather.7.cloned.1.call-done = f32[512,153,128]{2,0,1:T(8,128)} async-done(((f32[16,153,128]{2,0,1:T(8,128)}), f32[512,153,128]{2,0,1:T(8,128)}) %all-gather.7.cloned.1.call-update) | async-done | bytes 40108048 | tf_op jit(solution)/shard_map/all_gather | solution.py:22
  309.7 2.8 while.27
  309.7 1.4 constant_dynamic-slice_fusion.4
  312.5 1.7 fusion.38
  314.2 1.9 fusion.4
  316.1 1.8 copy.243
  318.7 1.7 convolution_bitcast_fusion.2
  322.8 136.4 %all-gather.3 = f32[512,153]{1,0:T(8,128)} all-gather(f32[16,153]{1,0:T(8,128)S(1)} %bitcast.226), channel_id=5, replica_groups=mesh['dp'=8,'ctx'=32] {'ctx'}, dimensions={0}, use_global_device_ids=true | all-gather | bytes 323136 | tf_op jit(solution)/shard_map/all_gather | solution.py:22
  464.3 219.4 %all-gather.9.cloned.1.call-done = f32[512,153,128]{2,0,1:T(8,128)} async-done(((f32[16,153,128]{2,0,1:T(8,128)}), f32[512,153,128]{2,0,1:T(8,128)}) %all-gather.9.cloned.1.call-update) | async-done | bytes 40108048 | tf_op jit(solution)/shard_map/all_gather | solution.py:22
  683.8 83.5 %while.28 = (s32[]{:T(128)}, f32[16,153,128]{2,1,0:T(8,128)S(1)}, f32[16,153]{1,0:T(8,128)S(1)}, s32[]{:T(128)}, f32[32,16,153,128]{3,1,0,2:T(8,128)}, /*index=5...) while((s32[]{:T(128)}, f32[16,153,128]{2,1,0:T(8,128)S(1)}, f32[16,153]{1,0:T(8,128)S(1)}, ...), condition=%wide.region_6.7_spmd, body=%wide.region_5.6_spmd.sunk | while | flops 315798 | bytes 6296419 | solution.py:31
  684.0 1.4 constant_dynamic-slice_fusion.5
  686.8 1.4 constant_dynamic-slice_fusion.5
  689.6 1.4 constant_dynamic-slice_fusion.5
  692.4 1.4 constant_dynamic-slice_fusion.5
  695.2 1.4 constant_dynamic-slice_fusion.5
  697.9 1.4 constant_dynamic-slice_fusion.5
  700.7 1.4 constant_dynamic-slice_fusion.5
  703.5 1.4 constant_dynamic-slice_fusion.5
  706.3 1.4 constant_dynamic-slice_fusion.5
  709.0 1.4 constant_dynamic-slice_fusion.5
  711.8 1.4 constant_dynamic-slice_fusion.5
  714.6 1.4 constant_dynamic-slice_fusion.5
  717.4 1.4 constant_dynamic-slice_fusion.5
  720.2 1.4 constant_dynamic-slice_fusion.5
  722.9 1.4 constant_dynamic-slice_fusion.5
  725.7 1.4 constant_dynamic-slice_fusion.5
  728.5 1.4 constant_dynamic-slice_fusion.5
  731.3 1.4 constant_dynamic-slice_fusion.5
  734.0 1.4 constant_dynamic-slice_fusion.5
  736.8 1.4 constant_dynamic-slice_fusion.5
  764.6 1.4 constant_dynamic-slice_fusion.5
  767.4 2.4 fusion.42
  771.2 1.9 fusion.24
  792.3 1.5 fusion.61
  794.7 6.8 collective-permute-start.1
  802.8 4.6 convolution_bitcast_fusion
  807.4 2.0 copy.259
  809.5 222.6 %reduce-scatter.2.cloned.1.call-done = f32[128,512]{0,1:T(8,128)} async-done(((f32[4096,512]{0,1:T(8,128)}), f32[128,512]{0,1:T(8,128)}) %reduce-scatter.2.cloned.1.call-update) | async-done | bytes 262160 | tf_op jit(solution)/shard_map/reduce_scatter | solution.py:117
  1033.8 1.5 collective-permute-start.3
  1036.9 5.4 collective-permute-done.3
  1042.3 3.1 collective-permute-start.4
  1045.4 4.6 fusion.2
  1050.0 1.4 collective-permute-done.4
  (393 shorter events, 98.2 us)
Async XLA Ops:
  7.2 7.7 copy-start.82
  7.2 302.3 %all-gather.7.cloned.1.call-start = ((), (), s32[]{:S(2)}) async-start(), calls=%async_computation.2 | async-start | bytes 41361408 | tf_op jit(solution)/shard_map/all_gather | solution.py:22
  8.4 6.5 copy-start.11
  11.4 5.5 collective-permute-start
  22.1 661.6 %all-gather.9.cloned.1.call-start = ((), (), s32[]{:S(2)}) async-start(), calls=%async_computation.3 | async-start | bytes 41361408 | tf_op jit(solution)/shard_map/all_gather | solution.py:22
  24.3 59.1 %copy-start.73 = (f32[128,128]{0,1:T(8,128)}, f32[128,128]{0,1:T(8,128)S(1)}, u32[]{:S(2)}) copy-start(f32[128,128]{0,1:T(8,128)S(1)} %fusion.76) | copy-start | bytes 196612
  82.0 227.5 %copy-start.1 = (bf16[16,153,128]{2,0,1:T(8,128)(2,1)}, bf16[16,153,128]{2,0,1:T(8,128)(2,1)S(1)}, u32[]{:S(2)}) copy-start(bf16[16,153,128]{2,0,1:T(8,128)(2,1)S(1)} %constant_dynamic-update-slice_fusion) | copy-start | bytes 1880068
  314.2 145.7 %copy-start.80 = (f32[128,16]{0,1:T(8,128)}, f32[128,16]{0,1:T(8,128)S(1)}, u32[]{:S(2)}) copy-start(f32[128,16]{0,1:T(8,128)S(1)} %get-tuple-element.278) | copy-start | bytes 24580
  317.9 714.1 %reduce-scatter.2.cloned.1.call-start = ((), (), s32[]{:S(2)}) async-start(), calls=%async_computation.1 | async-start | bytes 8650752 | tf_op jit(solution)/shard_map/reduce_scatter | solution.py:117
  321.7 137.5 %copy-start.74 = (f32[128,128]{0,1:T(8,128)S(1)}, f32[128,128]{0,1:T(8,128)}, u32[]{:S(2)}) copy-start(f32[128,128]{0,1:T(8,128)} %copy-done.73) | copy-start | bytes 196612
  773.1 18.3 %copy-start.5 = (f32[16,153,128]{2,0,1:T(8,128)}, f32[16,153,128]{2,0,1:T(8,128)S(1)}, u32[]{:S(2)}) copy-start(f32[16,153,128]{2,0,1:T(8,128)S(1)} %fusion.24) | copy-start | bytes 3760132
  773.9 4.9 copy-start.66
  773.9 4.9 copy-start.68
  773.9 4.9 copy-start.106
  774.7 5.5 copy-start.18
  774.7 5.5 copy-start.22
  774.7 5.5 copy-start.100
  776.0 5.5 copy-start.48
  776.1 5.5 copy-start.52
  776.1 5.5 copy-start.98
  777.4 5.5 copy-start.70
  777.4 5.5 copy-start.72
  777.4 5.5 copy-start.96
  777.5 6.8 copy-start.42
  777.5 6.8 copy-start.50
  777.5 6.8 copy-start.94
  778.8 6.8 copy-start.40
  778.8 6.8 copy-start.46
  778.8 6.8 copy-start.92
  778.8 7.4 copy-start.38
  778.9 7.4 copy-start.44
  778.9 7.4 copy-start.90
  780.2 7.4 copy-start.34
  780.2 7.4 copy-start.36
  780.2 7.4 copy-start.88
  780.2 8.6 copy-start.60
  780.3 8.6 copy-start.64
  780.3 8.6 copy-start.86
  781.6 8.6 copy-start.58
  781.6 8.6 copy-start.62
  781.6 8.6 copy-start.84
  781.6 10.4 copy-start.16
  781.6 10.4 copy-start.75
  794.7 8.1 collective-permute-start.1
  809.5 225.9 %copy-start.81 = (f32[128,16]{0,1:T(8,128)S(1)}, f32[128,16]{0,1:T(8,128)}, u32[]{:S(2)}) copy-start(f32[128,16]{0,1:T(8,128)} %copy-done.80) | copy-start | bytes 24580
  1032.0 1.7 collective-permute-start.2
  1033.8 8.4 collective-permute-start.3
  1042.3 9.1 collective-permute-start.4
  (73 other events, 128.7 us)
Sparse Core Ops, SparseCore 0:
  22.2 287.2 all-gather.6
  318.1 365.5 all-gather.8
  807.6 224.4 reduce-scatter.1
